TPU v7x, 128 devices: a whole 4x4x4 slice. The times are simulated.
128 devices in a mesh: sub: 16 (over y, z), grp: 8 (over x, core).
Axes of the slice: x: 4, y: 4, z: 4, core: 2. Of those that a mesh axis runs over, the one named last changes fastest.
Arguments:
- interior_res: bfloat16 [1024, 32, 256], P(('sub', 'grp')), may hold values from -6 to 6
- interface_res: bfloat16 [1024, 32, 512], P(('sub', 'grp')), may hold values from -6 to 6
- interior_inv: bfloat16 [1024, 256, 256], P(('sub', 'grp')), may hold values from -0.375 to 0.375
- coupling: bfloat16 [1024, 512, 256], P(('sub', 'grp')), may hold values from -0.375 to 0.375
- schur_inv: bfloat16 [1024, 512, 512], P(('sub', 'grp')), may hold values from -0.25 to 0.25
- coarse_inv: bfloat16 [512, 128, 128], P('grp'), may hold values from -0.5 to 0.5
- coarse_part: int32 [524288, 1], P(('sub', 'grp')), may hold values from 0 to 127; in each aligned block of 4096 rows (0 to 4095, 4096 to 8191, ...) at most 64 rows name the same one
- coarse_slot: int32 [524288], P(('sub', 'grp')), may hold values from 0 to 511
- live_count: int32 [1024], P(('sub', 'grp')), may hold values from 128 to 512
Outputs:
- interior_update: bfloat16 [1024, 32, 256], P(('sub', 'grp'))
- interface_update: bfloat16 [1024, 32, 512], P(('sub', 'grp'))
Inputs may be any that keep to these rules, and one draw needn't show every extreme that they name: `coarse_part`: in each device's aligned block of 4096 rows no section is named by more than 64 rows, a bound that some block reaches.
All inputs are finite; a program needn't handle non-finite values.
Results may differ from a plain program's by a relative error of at most 0.0076.
Values may be sent and summed in bfloat16 or wider, within the bound.
No kernel may reach another device: no remote copies, remote signals or barrier semaphores. Data moves between devices by JAX's collectives and lax.ppermute only.
A program may use at most 64 MiB of HBM per device.

v0:
```python
import math
import jax
import jax.numpy as jnp
from jax import lax
from jax.sharding import PartitionSpec as P


def coarse_apply(right_side, inverse_blocks):
    vec_count = right_side.shape[0]
    block_size = inverse_blocks.shape[1]
    reshaped = right_side.reshape(vec_count, -1, block_size)
    solved = jnp.einsum(
        "kbj,bij->kbi", reshaped, inverse_blocks, preferred_element_type=jnp.float32
    )
    return solved.reshape(vec_count, -1).astype(jnp.bfloat16)


def spread_cols(values, target, total):
    width = math.gcd(total, 512)

    def spread_one_block(number):
        columns = number * width + lax.iota(jnp.int32, width)
        table = (target[:, None] == columns[None, :]).astype(jnp.bfloat16)
        return jnp.dot(values, table, preferred_element_type=jnp.float32)

    blocks = lax.map(spread_one_block, jnp.arange(total // width, dtype=jnp.int32))
    return jnp.transpose(blocks, (1, 0, 2)).reshape(values.shape[0], total)


def pick_cols(values, wanted):
    count = wanted.shape[0]
    width = math.gcd(count, 512)
    source = lax.iota(jnp.int32, values.shape[1])

    def pick_one_block(number):
        chosen = lax.dynamic_slice_in_dim(wanted, number * width, width, 0)
        table = (source[:, None] == chosen[None, :]).astype(jnp.bfloat16)
        return jnp.dot(values, table, preferred_element_type=jnp.float32)

    blocks = lax.map(pick_one_block, jnp.arange(count // width, dtype=jnp.int32))
    return jnp.transpose(blocks, (1, 0, 2)).reshape(values.shape[0], count).astype(jnp.bfloat16)


def place_in_section(section_list, sections):
    rows_dev = section_list.shape[0]
    width = math.gcd(rows_dev, 128)
    section_hot = (section_list[:, None] == jnp.arange(sections, dtype=jnp.int32)[None, :]).astype(
        jnp.float32
    )
    hot_blocks = section_hot.reshape(rows_dev // width, width, sections)
    lower = (
        lax.broadcasted_iota(jnp.int32, (width, width), 0)
        >= lax.broadcasted_iota(jnp.int32, (width, width), 1)
    ).astype(jnp.float32)
    within = jnp.einsum("ij,bjs->bis", lower, hot_blocks, precision=lax.Precision.HIGHEST)
    totals = within[:, -1, :]
    before = jnp.cumsum(totals, axis=0) - totals
    counted = (within + before[:, None, :]).reshape(rows_dev, sections)
    return jnp.sum((counted - 1.0) * section_hot, axis=1).astype(jnp.int32)


def with_slots(flattened, slot_values):
    upper = (slot_values // 256).astype(jnp.bfloat16)[None, :]
    lower = (slot_values % 256).astype(jnp.bfloat16)[None, :]
    return jnp.concatenate([flattened, upper, lower], axis=0)


def read_slots(received, vec_count):
    upper = received[vec_count].astype(jnp.int32)
    lower = received[vec_count + 1].astype(jnp.int32)
    return (received[:vec_count], upper * 256 + lower)


def on_device(
    interior_res,
    interface_res,
    interior_inv,
    coupling,
    schur_inv,
    coarse_inv,
    coarse_part,
    coarse_slot,
    live_count,
):
    sub_count, vec_count, interior = interior_res.shape
    boundary = interface_res.shape[2]
    owners = lax.axis_size("grp")
    subgroups = lax.axis_size("sub")
    sections = owners * subgroups
    rows_dev = sub_count * boundary
    capacity = 2 * rows_dev // sections
    piece_size = rows_dev // 8
    per_owner = coarse_inv.shape[0] * coarse_inv.shape[1]
    interior_pre = jnp.einsum(
        "sij,skj->ski", interior_inv, interior_res, preferred_element_type=jnp.float32
    ).astype(jnp.bfloat16)
    condensed = interface_res.astype(jnp.float32) - jnp.einsum(
        "sbi,ski->skb", coupling, interior_pre, preferred_element_type=jnp.float32
    )
    alive_mask = (
        lax.broadcasted_iota(jnp.int32, (sub_count, 1, boundary), 2) < live_count[:, None, None]
    )
    condensed = jnp.where(alive_mask, condensed, 0.0).astype(jnp.bfloat16)
    section_list = coarse_part[:, 0]
    owner_list = section_list % owners
    piece_list = section_list // owners
    position = place_in_section(section_list, sections)
    flattened = jnp.transpose(condensed, (1, 0, 2)).reshape(vec_count, rows_dev)
    destination = owner_list * (subgroups * capacity) + piece_list * capacity + position
    owner_slot = piece_list * piece_size + coarse_slot
    outgoing = spread_cols(
        with_slots(flattened, owner_slot), destination, sections * capacity
    ).astype(jnp.bfloat16)
    received = lax.all_to_all(outgoing, "grp", split_axis=1, concat_axis=1, tiled=True)
    recv_rows, recv_slots = read_slots(received, vec_count)
    partial_sum = spread_cols(recv_rows, recv_slots, per_owner)
    summed = lax.psum(partial_sum, "sub")
    coarse_sol = coarse_apply(summed.astype(jnp.bfloat16), coarse_inv)
    replies = pick_cols(coarse_sol, recv_slots)
    returned = lax.all_to_all(replies, "grp", split_axis=1, concat_axis=1, tiled=True)
    correction = pick_cols(returned, destination)
    correction = jnp.transpose(correction.reshape(vec_count, sub_count, boundary), (1, 0, 2))
    local_term = jnp.einsum(
        "sbc,skc->skb", schur_inv, condensed, preferred_element_type=jnp.float32
    )
    interface_update = jnp.where(
        alive_mask, local_term + correction.astype(jnp.float32), 0.0
    ).astype(jnp.bfloat16)
    extended = interior_res.astype(jnp.float32) - jnp.einsum(
        "sbi,skb->ski", coupling, interface_update, preferred_element_type=jnp.float32
    )
    interior_update = jnp.einsum(
        "sij,skj->ski",
        interior_inv,
        extended.astype(jnp.bfloat16),
        preferred_element_type=jnp.float32,
    ).astype(jnp.bfloat16)
    return (interior_update, interface_update)


def solution(mesh):
    in_specs = (
        P(("sub", "grp"), None, None),
        P(("sub", "grp"), None, None),
        P(("sub", "grp"), None, None),
        P(("sub", "grp"), None, None),
        P(("sub", "grp"), None, None),
        P("grp", None, None),
        P(("sub", "grp"), None),
        P(("sub", "grp")),
        P(("sub", "grp")),
    )
    out_specs = (P(("sub", "grp"), None, None), P(("sub", "grp"), None, None))
    return jax.shard_map(
        on_device, mesh=mesh, in_specs=in_specs, out_specs=out_specs, check_vma=False
    )
```

profile of v0, /device:TPU:1, one launch (start us, length us, event | category | flops | bytes accessed | tf_op | source)
XLA Modules:
  0.0 473.6 jit_solution(12313746118868401771)
XLA Ops:
  10.9 69.0 %while.46 = (s32[]{:T(128)}, bf16[16,34,512]{2,1,0:T(8,128)(2,1)}, s32[4096]{0:T(1024)}, s32[16]{0:T(128)S(1)}, bf16[34,4096]{1,0:T(8,128)(2,1)}, /*index=5*/s32[1]{0:T(128)}) while((s32[]{:T(128)}, bf16[16,34,512]{2,1,0:T(8,128)(2,1)}, s32[4096]{0:T(1024)}, s32[16]{0:T(128)S(1)}, bf16[34,4096]{1,0:T(8,128)(2,1)}, ...), condition=%wide.region_3.4_spmd.clone, body=%wide.region_2.3_spmd.sunk.clone | while | flops 144704000 | bytes 430689 | solution.py:26
  86.2 5.8 %all-to-all-start = ((bf16[34,8,1024]{2,0,1:T(8,128)(2,1)}), bf16[34,8,1024]{2,0,1:T(8,128)(2,1)}, u32[]{:S(2)}, u32[]{:S(2)}) async-start(bf16[34,8,1024]{2,0,1:T(8,128)(2,1)} %copy.27), calls=%async_computation | async-start | bytes 1310720 | tf_op jit(solution)/shard_map/all_to_all | solution.py:114
  92.8 10.0 %all-to-all-done = bf16[34,8,1024]{2,0,1:T(8,128)(2,1)} async-done(((bf16[34,8,1024]{2,0,1:T(8,128)(2,1)}), bf16[34,8,1024]{2,0,1:T(8,128)(2,1)}, u32[]{:S(2)}, u32[]{:S(2)}) %all-to-all-start) | async-done | bytes 557088 | tf_op jit(solution)/shard_map/all_to_all | solution.py:114
  106.5 88.7 %while.47 = (s32[]{:T(128)}, f32[16,32,512]{2,1,0:T(8,128)}, s32[8192]{0:T(1024)}, s32[16]{0:T(128)S(1)}, bf16[32,8192]{1,0:T(8,128)(2,1)}, /*index=5*/s32[1]{0:T(128)}) while((s32[]{:T(128)}, f32[16,32,512]{2,1,0:T(8,128)}, s32[8192]{0:T(1024)}, s32[16]{0:T(128)S(1)}, bf16[32,8192]{1,0:T(8,128)(2,1)}, /*index=5*/s32[1]{0:T(128)}) %tuple.96), condition=%wide.region_5.6_spmd.clone, body=%wide.region_4.5_spmd.sunk.clone | while | flops 272630272 | bytes 627297 | solution.py:26
  107.7 4.4 fusion.97
  113.2 4.4 fusion.97
  118.8 4.4 fusion.97
  124.3 4.4 fusion.97
  129.9 4.4 fusion.97
  135.4 4.4 fusion.97
  140.9 4.4 fusion.97
  146.5 4.4 fusion.97
  152.0 4.4 fusion.97
  157.6 4.4 fusion.97
  168.7 4.4 fusion.97
  174.2 4.4 fusion.97
  179.8 4.4 fusion.97
  185.3 4.4 fusion.97
  190.9 4.4 fusion.97
  197.6 76.3 %all-reduce.1 = bf16[32,8192]{1,0:T(8,128)(2,1)} all-reduce(f32[32,8192]{1,0:T(8,128)} %bitcast.120), channel_id=1, replica_groups=mesh['sub'=16,'grp'=8] {'sub'}, use_global_device_ids=true, to_apply=%region_6.7 | all-reduce | flops 262144 | bytes 1572864 | tf_op jit(solution)/shard_map/psum | solution.py:117
  277.0 101.6 %while.48 = (s32[]{:T(128)}, bf16[16,32,512]{2,1,0:T(8,128)(2,1)}, s32[16]{0:T(128)S(1)}, s32[8192]{0:T(1024)}, bf16[32,8192]{1,0:T(8,128)(2,1)}, /*index=5*/s32[1]{0:T(128)}) while((s32[]{:T(128)}, bf16[16,32,512]{2,1,0:T(8,128)(2,1)}, s32[16]{0:T(128)S(1)}, s32[8192]{0:T(1024)}, bf16[32,8192]{1,0:T(8,128)(2,1)}, ...), condition=%wide.region_8.9_spmd.clone.clone, body=%wide.region_7.8_spmd.clone.sunk.clone | while | flops 272629760 | bytes 596611 | solution.py:40
  384.9 19.1 %all-to-all-start.1 = ((bf16[32,8,1024]{2,0,1:T(8,128)(2,1)}), bf16[32,8,1024]{2,0,1:T(8,128)(2,1)}, u32[]{:S(2)}, u32[]{:S(2)}) async-start(bf16[32,8,1024]{2,0,1:T(8,128)(2,1)} %copy.33), calls=%async_computation.1 | async-start | bytes 1048576 | tf_op jit(solution)/shard_map/all_to_all | solution.py:120
  404.0 9.5 %all-to-all-done.1 = bf16[32,8,1024]{2,0,1:T(8,128)(2,1)} async-done(((bf16[32,8,1024]{2,0,1:T(8,128)(2,1)}), bf16[32,8,1024]{2,0,1:T(8,128)(2,1)}, u32[]{:S(2)}, u32[]{:S(2)}) %all-to-all-start.1) | async-done | bytes 524320 | tf_op jit(solution)/shard_map/all_to_all | solution.py:120
  415.3 50.9 %while.49 = (s32[]{:T(128)}, bf16[8,32,512]{2,1,0:T(8,128)(2,1)}, s32[8]{0:T(128)S(1)}, s32[4096]{0:T(1024)}, bf16[32,8192]{1,0:T(8,128)(2,1)}, /*index=5*/s32[1]{0:T(128)}) while((s32[]{:T(128)}, bf16[8,32,512]{2,1,0:T(8,128)(2,1)}, s32[8]{0:T(128)S(1)}, s32[4096]{0:T(1024)}, bf16[32,8192]{1,0:T(8,128)(2,1)}, ...), condition=%wide.region_10.11_spmd.clone.clone, body=%wide.region_9.10_spmd.clone.sunk.clone | while | flops 272629760 | bytes 596611 | solution.py:40
  (201 shorter events, 251.1 us)
Async XLA Ops:
  0.6 273.3 %copy-start = (bf16[64,128,128]{2,1,0:T(8,128)(2,1)S(1)}, bf16[64,128,128]{2,1,0:T(8,128)(2,1)}, u32[]{:S(2)}) copy-start(bf16[64,128,128]{2,1,0:T(8,128)(2,1)} %param.22) | copy-start | bytes 6291460
  0.6 1.8 copy-start.3
  0.7 3.1 copy-start.5
  0.7 4.4 copy-start.6
  0.7 5.0 %copy-start.1 = (bf16[8,256,256]{2,1,0:T(8,128)(2,1)S(1)}, bf16[8,256,256]{2,1,0:T(8,128)(2,1)}, u32[]{:S(2)}) copy-start(bf16[8,256,256]{2,1,0:T(8,128)(2,1)} %param.19) | copy-start | bytes 3145732
  0.7 5.0 %copy-start.2 = (bf16[8,32,256]{2,1,0:T(8,128)(2,1)S(1)}, bf16[8,32,256]{2,1,0:T(8,128)(2,1)}, u32[]{:S(2)}) copy-start(bf16[8,32,256]{2,1,0:T(8,128)(2,1)} %param.17) | copy-start | bytes 393220
  86.2 16.6 %all-to-all-start = ((bf16[34,8,1024]{2,0,1:T(8,128)(2,1)}), bf16[34,8,1024]{2,0,1:T(8,128)(2,1)}, u32[]{:S(2)}, u32[]{:S(2)}) async-start(bf16[34,8,1024]{2,0,1:T(8,128)(2,1)} %copy.27), calls=%async_computation | async-start | bytes 1310720 | tf_op jit(solution)/shard_map/all_to_all | solution.py:114
  384.9 28.5 %all-to-all-start.1 = ((bf16[32,8,1024]{2,0,1:T(8,128)(2,1)}), bf16[32,8,1024]{2,0,1:T(8,128)(2,1)}, u32[]{:S(2)}, u32[]{:S(2)}) async-start(bf16[32,8,1024]{2,0,1:T(8,128)(2,1)} %copy.33), calls=%async_computation.1 | async-start | bytes 1048576 | tf_op jit(solution)/shard_map/all_to_all | solution.py:120
  415.3 50.9 %copy-start.4 = (pred[8,512]{1,0:T(8,128)(4,1)S(1)}, pred[8,512]{1,0:T(8,128)(4,1)}, u32[]{:S(2)}) copy-start(pred[8,512]{1,0:T(8,128)(4,1)} %iota_compare_fusion.17) | copy-start | bytes 12292
where the time goes:
time: 477 us; the launch traced here: 474 us
  matrix products  238 us (50%)
  blocking collectives  76.3 us (16%)
  local copies, waits for them, and re-layouts  71.9 us (15%)
  loops' own time  35.1 us (7%)
  starting transfers between devices  24.8 us (5%)
  waiting for transfers between devices  19.5 us (4%)
  other arithmetic  7.01 us (1%)
    dot_general x32, matrix products, spread_one_block(): return jnp.dot(values, table, preferred_element_type=jnp.float32)  119 us
    dot_general x24, matrix products, pick_one_block(): return jnp.dot(values, table, preferred_element_type=jnp.float32)  105 us
    psum x1, blocking collectives, on_device(): summed = lax.psum(partial_sum, 'sub')  76.3 us
    dynamic_slice x48, local copies, waits for them, and re-layouts, spread_cols(): lax.map(spread_one_block, jnp.arange(total // width, dtype=jnp.int32))  28 us
    another operation x2, loops' own time, spread_cols(): lax.map(spread_one_block, jnp.arange(total // width, dtype=jnp.int32))  19.7 us
    all_to_all x1, starting transfers between devices, on_device(): lax.all_to_all(replies, 'grp', split_axis=1, concat_axis=1, tiled=True)  19.1 us
    dynamic_slice x24, local copies, waits for them, and re-layouts, pick_one_block(): chosen = lax.dynamic_slice_in_dim(wanted, number * width, width, 0)  18.2 us
    another operation x2, loops' own time, pick_cols(): lax.map(pick_one_block, jnp.arange(count // width, dtype=jnp.int32))  15.4 us
  transfers between devices with their start and end apart: 2, of which 2 were waited for; matrix products, arithmetic and copies ran while one was open for 0% of the time, Pallas kernels for 0%

commit v1 on v0

--- a/solution.py
+++ b/solution.py
@@ -114,7 +114,9 @@
     received = lax.all_to_all(outgoing, "grp", split_axis=1, concat_axis=1, tiled=True)
     recv_rows, recv_slots = read_slots(received, vec_count)
     partial_sum = spread_cols(recv_rows, recv_slots, per_owner)
-    summed = lax.psum(partial_sum, "sub")
+    summed = partial_sum
+    for hop in (1, 2, 4, 8):
+        summed = summed + lax.ppermute(summed, "sub", [(dev, dev ^ hop) for dev in range(16)])
     coarse_sol = coarse_apply(summed.astype(jnp.bfloat16), coarse_inv)
     replies = pick_cols(coarse_sol, recv_slots)
     returned = lax.all_to_all(replies, "grp", split_axis=1, concat_axis=1, tiled=True)

time: 477 us -> 486 us (1.019)
  waiting for transfers between devices: 19.5 us -> 105 us
  blocking collectives: 76.3 us -> 0 us
    ppermute x0 -> x4, waiting for transfers between devices: none -> 84.7 us  [on_device(): lax.ppermute(summed, 'sub', [(dev, dev ^ hop) for dev in range(16)])]
    psum x1 -> x0, blocking collectives: 76.3 us -> none  [on_device(): summed = lax.psum(partial_sum, 'sub')]
    all_to_all x1, starting transfers between devices: 19.1 us -> 8.13 us  [on_device(): lax.all_to_all(replies, 'grp', split_axis=1, concat_axis=1, tiled=True)]
    ppermute x0 -> x4, starting transfers between devices: none -> 9.32 us  [on_device(): lax.ppermute(summed, 'sub', [(dev, dev ^ hop) for dev in range(16)])]
  transfers between devices with their start and end apart: 2 -> 6, of which waited for: 2 -> 6; matrix products, arithmetic and copies ran while one was open for 0% -> 0% of each run, Pallas kernels for 0% -> 0%
where the time goes in v1:
time: 486 us; the launch traced here: 482 us
  matrix products  239 us (49%)
  waiting for transfers between devices  105 us (22%)
  local copies, waits for them, and re-layouts  70.5 us (15%)
  loops' own time  34.9 us (7%)
  starting transfers between devices  23.2 us (5%)
  other arithmetic  8.32 us (2%)
    dot_general x32, matrix products, spread_one_block(): return jnp.dot(values, table, preferred_element_type=jnp.float32)  119 us
    dot_general x24, matrix products, pick_one_block(): return jnp.dot(values, table, preferred_element_type=jnp.float32)  105 us
    ppermute x4, waiting for transfers between devices, on_device(): lax.ppermute(summed, 'sub', [(dev, dev ^ hop) for dev in range(16)])  84.7 us
    dynamic_slice x48, local copies, waits for them, and re-layouts, spread_cols(): lax.map(spread_one_block, jnp.arange(total // width, dtype=jnp.int32))  27.6 us
    another operation x2, loops' own time, spread_cols(): lax.map(spread_one_block, jnp.arange(total // width, dtype=jnp.int32))  20.8 us
    dynamic_slice x24, local copies, waits for them, and re-layouts, pick_one_block(): chosen = lax.dynamic_slice_in_dim(wanted, number * width, width, 0)  18.2 us
    another operation x2, loops' own time, pick_cols(): lax.map(pick_one_block, jnp.arange(count // width, dtype=jnp.int32))  14.2 us
    all_to_all x1, waiting for transfers between devices, on_device(): lax.all_to_all(outgoing, 'grp', split_axis=1, concat_axis=1, tiled=True)  10.9 us
  transfers between devices with their start and end apart: 6, of which 6 were waited for; matrix products, arithmetic and copies ran while one was open for 0% of the time, Pallas kernels for 0%

profile of v1, /device:TPU:1, one launch (start us, length us, event | category | flops | bytes accessed | tf_op | source)
XLA Modules:
  0.0 481.8 jit_solution(1503422883917202910)
XLA Ops:
  10.9 69.0 %while.46 = (s32[]{:T(128)}, bf16[16,34,512]{2,1,0:T(8,128)(2,1)}, s32[4096]{0:T(1024)}, s32[16]{0:T(128)S(1)}, bf16[34,4096]{1,0:T(8,128)(2,1)}, /*index=5*/s32[1]{0:T(128)}) while((s32[]{:T(128)}, bf16[16,34,512]{2,1,0:T(8,128)(2,1)}, s32[4096]{0:T(1024)}, s32[16]{0:T(128)S(1)}, bf16[34,4096]{1,0:T(8,128)(2,1)}, ...), condition=%wide.region_3.4_spmd.clone, body=%wide.region_2.3_spmd.sunk.clone | while | flops 144704000 | bytes 430689 | solution.py:26
  86.2 5.8 %all-to-all-start = ((bf16[34,8,1024]{2,0,1:T(8,128)(2,1)}), bf16[34,8,1024]{2,0,1:T(8,128)(2,1)}, u32[]{:S(2)}, u32[]{:S(2)}) async-start(bf16[34,8,1024]{2,0,1:T(8,128)(2,1)} %copy.27), calls=%async_computation | async-start | bytes 1310720 | tf_op jit(solution)/shard_map/all_to_all | solution.py:114
  92.0 10.9 %all-to-all-done = bf16[34,8,1024]{2,0,1:T(8,128)(2,1)} async-done(((bf16[34,8,1024]{2,0,1:T(8,128)(2,1)}), bf16[34,8,1024]{2,0,1:T(8,128)(2,1)}, u32[]{:S(2)}, u32[]{:S(2)}) %all-to-all-start) | async-done | bytes 557088 | tf_op jit(solution)/shard_map/all_to_all | solution.py:114
  106.5 90.2 %while.47 = (s32[]{:T(128)}, f32[16,32,512]{2,1,0:T(8,128)}, s32[8192]{0:T(1024)}, s32[16]{0:T(128)S(1)}, bf16[32,8192]{1,0:T(8,128)(2,1)}, /*index=5*/s32[1]{0:T(128)}) while((s32[]{:T(128)}, f32[16,32,512]{2,1,0:T(8,128)}, s32[8192]{0:T(1024)}, s32[16]{0:T(128)S(1)}, bf16[32,8192]{1,0:T(8,128)(2,1)}, /*index=5*/s32[1]{0:T(128)}) %tuple.96), condition=%wide.region_5.6_spmd.clone, body=%wide.region_4.5_spmd.sunk.clone | while | flops 272630272 | bytes 627297 | solution.py:26
  113.4 4.4 fusion.99
  119.0 4.4 fusion.99
  124.7 4.4 fusion.99
  130.3 4.4 fusion.99
  135.9 4.4 fusion.99
  141.6 4.4 fusion.99
  147.2 4.4 fusion.99
  158.5 4.4 fusion.99
  169.7 4.4 fusion.99
  175.4 4.4 fusion.99
  186.6 4.4 fusion.99
  192.3 4.4 fusion.99
  199.7 22.5 %collective-permute-done = f32[32,8192]{1,0:T(8,128)S(1)} collective-permute-done((f32[32,8192]{1,0:T(8,128)S(1)}, f32[32,8192]{1,0:T(8,128)S(1)}, u32[]{:S(2)}, u32[]{:S(2)}) %collective-permute-start) | collective-permute-done | bytes 1048608 | tf_op jit(solution)/shard_map/ppermute | solution.py:119
  225.6 21.7 %collective-permute-done.1 = f32[32,8192]{1,0:T(8,128)S(1)} collective-permute-done((f32[32,8192]{1,0:T(8,128)S(1)}, f32[32,8192]{1,0:T(8,128)S(1)}, u32[]{:S(2)}, u32[]{:S(2)}) %collective-permute-start.1) | collective-permute-done | bytes 1048608 | tf_op jit(solution)/shard_map/ppermute | solution.py:119
  248.8 21.0 %collective-permute-done.2 = f32[32,8192]{1,0:T(8,128)S(1)} collective-permute-done((f32[32,8192]{1,0:T(8,128)S(1)}, f32[32,8192]{1,0:T(8,128)S(1)}, u32[]{:S(2)}, u32[]{:S(2)}) %collective-permute-start.2) | collective-permute-done | bytes 1048608 | tf_op jit(solution)/shard_map/ppermute | solution.py:119
  274.7 19.5 %collective-permute-done.3 = f32[32,8192]{1,0:T(8,128)} collective-permute-done((f32[32,8192]{1,0:T(8,128)}, f32[32,8192]{1,0:T(8,128)}, u32[]{:S(2)}, u32[]{:S(2)}) %collective-permute-start.3) | collective-permute-done | bytes 1048608 | tf_op jit(solution)/shard_map/ppermute | solution.py:119
  297.8 99.9 %while.48 = (s32[]{:T(128)}, bf16[16,32,512]{2,1,0:T(8,128)(2,1)}, s32[16]{0:T(128)S(1)}, s32[8192]{0:T(1024)}, bf16[32,8192]{1,0:T(8,128)(2,1)}, /*index=5*/s32[1]{0:T(128)}) while((s32[]{:T(128)}, bf16[16,32,512]{2,1,0:T(8,128)(2,1)}, s32[16]{0:T(128)S(1)}, s32[8192]{0:T(1024)}, bf16[32,8192]{1,0:T(8,128)(2,1)}, ...), condition=%wide.region_7.8_spmd.clone.clone, body=%wide.region_6.7_spmd.clone.sunk.clone | while | flops 272629760 | bytes 596611 | solution.py:40
  404.0 8.1 %all-to-all-start.1 = ((bf16[32,8,1024]{2,0,1:T(8,128)(2,1)}), bf16[32,8,1024]{2,0,1:T(8,128)(2,1)}, u32[]{:S(2)}, u32[]{:S(2)}) async-start(bf16[32,8,1024]{2,0,1:T(8,128)(2,1)} %copy.33), calls=%async_computation.1 | async-start | bytes 1048576 | tf_op jit(solution)/shard_map/all_to_all | solution.py:122
  412.1 9.5 %all-to-all-done.1 = bf16[32,8,1024]{2,0,1:T(8,128)(2,1)} async-done(((bf16[32,8,1024]{2,0,1:T(8,128)(2,1)}), bf16[32,8,1024]{2,0,1:T(8,128)(2,1)}, u32[]{:S(2)}, u32[]{:S(2)}) %all-to-all-start.1) | async-done | bytes 524320 | tf_op jit(solution)/shard_map/all_to_all | solution.py:122
  423.5 50.9 %while.49 = (s32[]{:T(128)}, bf16[8,32,512]{2,1,0:T(8,128)(2,1)}, s32[8]{0:T(128)S(1)}, s32[4096]{0:T(1024)}, bf16[32,8192]{1,0:T(8,128)(2,1)}, /*index=5*/s32[1]{0:T(128)}) while((s32[]{:T(128)}, bf16[8,32,512]{2,1,0:T(8,128)(2,1)}, s32[8]{0:T(128)S(1)}, s32[4096]{0:T(1024)}, bf16[32,8192]{1,0:T(8,128)(2,1)}, ...), condition=%wide.region_9.10_spmd.clone.clone, body=%wide.region_8.9_spmd.clone.sunk.clone | while | flops 272629760 | bytes 596611 | solution.py:40
  (211 shorter events, 274.2 us)
Async XLA Ops:
  0.6 293.6 %copy-start = (bf16[64,128,128]{2,1,0:T(8,128)(2,1)S(1)}, bf16[64,128,128]{2,1,0:T(8,128)(2,1)}, u32[]{:S(2)}) copy-start(bf16[64,128,128]{2,1,0:T(8,128)(2,1)} %param.22) | copy-start | bytes 6291460
  0.6 1.8 copy-start.3
  0.7 3.1 copy-start.5
  0.7 4.4 copy-start.6
  0.7 5.0 %copy-start.1 = (bf16[8,256,256]{2,1,0:T(8,128)(2,1)S(1)}, bf16[8,256,256]{2,1,0:T(8,128)(2,1)}, u32[]{:S(2)}) copy-start(bf16[8,256,256]{2,1,0:T(8,128)(2,1)} %param.19) | copy-start | bytes 3145732
  0.7 5.0 %copy-start.2 = (bf16[8,32,256]{2,1,0:T(8,128)(2,1)S(1)}, bf16[8,32,256]{2,1,0:T(8,128)(2,1)}, u32[]{:S(2)}) copy-start(bf16[8,32,256]{2,1,0:T(8,128)(2,1)} %param.17) | copy-start | bytes 393220
  86.2 16.6 %all-to-all-start = ((bf16[34,8,1024]{2,0,1:T(8,128)(2,1)}), bf16[34,8,1024]{2,0,1:T(8,128)(2,1)}, u32[]{:S(2)}, u32[]{:S(2)}) async-start(bf16[34,8,1024]{2,0,1:T(8,128)(2,1)} %copy.27), calls=%async_computation | async-start | bytes 1310720 | tf_op jit(solution)/shard_map/all_to_all | solution.py:114
  198.0 24.2 %collective-permute-start = (f32[32,8192]{1,0:T(8,128)S(1)}, f32[32,8192]{1,0:T(8,128)S(1)}, u32[]{:S(2)}, u32[]{:S(2)}) collective-permute-start(f32[32,8192]{1,0:T(8,128)S(1)} %bitcast.118), channel_id=1, source_target_pairs={{0,8},{8,0},{16,24},{24,16},{32,40},{40,32},{48,56},{56,48},{64,72... | collective-permute-start | bytes 3145736 | tf_op jit(solution)/shard_map/ppermute | solution.py:119
  222.3 25.0 %collective-permute-start.1 = (f32[32,8192]{1,0:T(8,128)S(1)}, f32[32,8192]{1,0:T(8,128)S(1)}, u32[]{:S(2)}, u32[]{:S(2)}) collective-permute-start(f32[32,8192]{1,0:T(8,128)S(1)} %add.102), channel_id=1, source_target_pairs={{0,16},{8,24},{16,0},{24,8},{32,48},{40,56},{48,32},{56,40},{64,80... | collective-permute-start | bytes 3145736 | tf_op jit(solution)/shard_map/ppermute | solution.py:119
  247.4 22.4 %collective-permute-start.2 = (f32[32,8192]{1,0:T(8,128)S(1)}, f32[32,8192]{1,0:T(8,128)S(1)}, u32[]{:S(2)}, u32[]{:S(2)}) collective-permute-start(f32[32,8192]{1,0:T(8,128)S(1)} %add.103), channel_id=1, source_target_pairs={{0,32},{8,40},{16,48},{24,56},{32,0},{40,8},{48,16},{56,24},{64,96... | collective-permute-start | bytes 3145736 | tf_op jit(solution)/shard_map/ppermute | solution.py:119
  270.9 23.3 %collective-permute-start.3 = (f32[32,8192]{1,0:T(8,128)}, f32[32,8192]{1,0:T(8,128)}, u32[]{:S(2)}, u32[]{:S(2)}) collective-permute-start(f32[32,8192]{1,0:T(8,128)} %add.104), channel_id=1, source_target_pairs={{0,64},{8,72},{16,80},{24,88},{32,96},{40,104},{48,112},{56,120},{... | collective-permute-start | bytes 3145736 | tf_op jit(solution)/shard_map/ppermute | solution.py:119
  404.0 17.6 %all-to-all-start.1 = ((bf16[32,8,1024]{2,0,1:T(8,128)(2,1)}), bf16[32,8,1024]{2,0,1:T(8,128)(2,1)}, u32[]{:S(2)}, u32[]{:S(2)}) async-start(bf16[32,8,1024]{2,0,1:T(8,128)(2,1)} %copy.33), calls=%async_computation.1 | async-start | bytes 1048576 | tf_op jit(solution)/shard_map/all_to_all | solution.py:122
  423.5 50.9 %copy-start.4 = (pred[8,512]{1,0:T(8,128)(4,1)S(1)}, pred[8,512]{1,0:T(8,128)(4,1)}, u32[]{:S(2)}) copy-start(pred[8,512]{1,0:T(8,128)(4,1)} %iota_compare_fusion.17) | copy-start | bytes 12292
